TPU v7x, 32 devices: a whole 2x2x4 slice. The times are simulated.
32 devices in a mesh: seq: 4 (over x, core), fsdp: 8 (over z, y).
Axes of the slice: x: 2, y: 2, z: 4, core: 2. Of those that a mesh axis runs over, the one named last changes fastest.
Arguments:
- tokens: bfloat16 [2, 8, 1024, 1024], P(None, 'fsdp', 'seq'), may hold values from -6 to 6
- positions: int32 [2, 8, 1024], P(None, 'fsdp'), may hold values from 0 to 1023, as said below
- input_gain: bfloat16 [1024], P(('seq', 'fsdp')), may hold values from 0.5 to 1.5
- post_gain: bfloat16 [1024], P(('seq', 'fsdp')), may hold values from 0.5 to 1.5
- query_gain: bfloat16 [128], P(('seq', 'fsdp')), may hold values from 0.5 to 1.5
- key_gain: bfloat16 [128], P(('seq', 'fsdp')), may hold values from 0.5 to 1.5
- w_query: bfloat16 [1024, 2048], P(('seq', 'fsdp')), may hold values from -0.1875 to 0.1875
- w_key: bfloat16 [1024, 1024], P(('seq', 'fsdp')), may hold values from -0.1875 to 0.1875
- w_value: bfloat16 [1024, 1024], P(('seq', 'fsdp')), may hold values from -0.1875 to 0.1875
- w_out: bfloat16 [2048, 1024], P(('seq', 'fsdp')), may hold values from -1.5 to 1.5
- w_gate: bfloat16 [1024, 3072], P(('seq', 'fsdp')), may hold values from -0.1875 to 0.1875
- w_up: bfloat16 [1024, 3072], P(('seq', 'fsdp')), may hold values from -0.1875 to 0.1875
- w_down: bfloat16 [3072, 1024], P(('seq', 'fsdp')), may hold values from -0.109375 to 0.109375
- cotangent: bfloat16 [2, 8, 1024, 1024], P(None, 'fsdp', 'seq'), may hold values from -6 to 6
Outputs:
- block_out: bfloat16 [2, 8, 1024, 1024], P(None, 'fsdp', 'seq')
- tokens_grad: float32 [2, 8, 1024, 1024], P(None, 'fsdp', 'seq')
- input_gain_grad: float32 [1024], P(('seq', 'fsdp'))
- post_gain_grad: float32 [1024], P(('seq', 'fsdp'))
- query_gain_grad: float32 [128], P(('seq', 'fsdp'))
- key_gain_grad: float32 [128], P(('seq', 'fsdp'))
- w_query_grad: float32 [1024, 2048], P(('seq', 'fsdp'))
- w_key_grad: float32 [1024, 1024], P(('seq', 'fsdp'))
- w_value_grad: float32 [1024, 1024], P(('seq', 'fsdp'))
- w_out_grad: float32 [2048, 1024], P(('seq', 'fsdp'))
- w_gate_grad: float32 [1024, 3072], P(('seq', 'fsdp'))
- w_up_grad: float32 [1024, 3072], P(('seq', 'fsdp'))
- w_down_grad: float32 [3072, 1024], P(('seq', 'fsdp'))
Inputs may be any that keep to these rules, and one draw needn't show every extreme that they name: In each sequence the positions are a permutation of 0 to 1023 made of runs of 128 consecutive positions, each run starting at a multiple of 128; the order of the runs is drawn at random for each sequence.
All inputs are finite; a program needn't handle non-finite values.
Results may differ from a plain program's by a relative error of at most 0.02.
Values may be sent and summed in bfloat16 or wider, within the bound.
A program may use at most 160 MiB of HBM per device.

v0:
```python
import jax
import jax.numpy as jnp
from jax import lax
from jax.sharding import PartitionSpec as P

HEADS = 16
KV_HEADS = 8
HEAD_DIM = 128
EPSILON = 1e-06
ROPE_BASE = 1000000.0
NEGATIVE = -1e30
F32 = jnp.float32
BF16 = jnp.bfloat16


def inverse_root(values):
    return lax.rsqrt(jnp.mean(values * values, axis=-1, keepdims=True) + EPSILON)


def rope_tables(token_pos):
    half_width = HEAD_DIM // 2
    frequency = ROPE_BASE ** (-(jnp.arange(half_width, dtype=F32) * 2.0 / HEAD_DIM))
    angles = token_pos.astype(F32)[:, None] * frequency[None, :]
    cosine = jnp.cos(angles)
    sine = jnp.sin(angles)
    return (
        jnp.concatenate([cosine, cosine], axis=-1)[:, None, :],
        jnp.concatenate([sine, sine], axis=-1)[:, None, :],
    )


def rotate(values, cosine, sine):
    half_width = values.shape[-1] // 2
    turned = jnp.concatenate([-values[..., half_width:], values[..., :half_width]], axis=-1)
    return values * cosine + turned * sine


def rotate_back(grads, cosine, sine):
    half_width = grads.shape[-1] // 2
    scaled = grads * sine
    turned = jnp.concatenate([scaled[..., half_width:], -scaled[..., :half_width]], axis=-1)
    return grads * cosine + turned


def norm_back(grads, values, inverse, gain):
    scaled = grads * gain
    return inverse * scaled - values * inverse**3 * jnp.mean(
        scaled * values, axis=-1, keepdims=True
    )


def mul(eq, left, right):
    return jnp.einsum(eq, left, right, preferred_element_type=F32)


def sum_scatter(part, axis):
    return lax.psum_scatter(part.astype(BF16), axis, scatter_dimension=0, tiled=True).astype(F32)


def slice_weights(item, ways):
    rows = item.shape[0]
    return item.reshape(rows, ways, -1).transpose(1, 0, 2)


def plain_body(
    tokens,
    positions,
    g_in,
    g_post,
    g_query,
    g_key,
    w_query,
    w_key,
    w_value,
    w_out,
    w_gate,
    w_up,
    w_down,
    cotangent,
):
    ways = lax.axis_size("seq")
    heads, kv_heads = (HEADS // ways, KV_HEADS // ways)
    micro, rows, width = (tokens.shape[0], tokens.shape[2], tokens.shape[3])
    length = positions.shape[2]
    everyone = ("seq", "fsdp")
    gains = [
        lax.all_gather(item, everyone, axis=0, tiled=True).astype(F32)
        for item in (g_in, g_post, g_query, g_key)
    ]
    gain_in, gain_post, gain_query, gain_key = gains

    def spread(*items):
        packed = jnp.concatenate([slice_weights(item, ways) for item in items], axis=2)
        packed = lax.all_to_all(packed, "seq", 0, 0, tiled=True)
        packed = lax.all_gather(packed, "fsdp", axis=1, tiled=True)
        packed = packed.reshape(-1, packed.shape[2])
        sizes = [item.shape[1] // ways for item in items]
        cuts = [sum(sizes[: at + 1]) for at in range(len(sizes) - 1)]
        return jnp.split(packed, cuts, axis=1)

    wq, wk, wv = spread(w_query, w_key, w_value)
    wo = lax.all_gather(w_out, "fsdp", axis=0, tiled=True)
    wg, wu = spread(w_gate, w_up)
    wd = lax.all_gather(w_down, "fsdp", axis=0, tiled=True)
    scale = HEAD_DIM ** (-0.5)

    def gather_rows(item):
        return lax.all_gather(item, "seq", axis=0, tiled=True)

    grads = None
    outs, token_grads = ([], [])
    for at in range(micro):
        inputs = tokens[at, 0].astype(F32)
        pos = positions[at, 0]
        cosine, sine = rope_tables(pos)
        allowed = pos[None, :] <= pos[:, None]
        inv_in = inverse_root(inputs)
        normed = gather_rows((inputs * inv_in * gain_in).astype(BF16))
        q_raw = mul("td,df->tf", normed, wq).reshape(length, heads, HEAD_DIM)
        k_raw = mul("td,df->tf", normed, wk).reshape(length, kv_heads, HEAD_DIM)
        value = mul("td,df->tf", normed, wv).astype(BF16).reshape(length, kv_heads, HEAD_DIM)
        inv_q, inv_k = (inverse_root(q_raw), inverse_root(k_raw))
        query = rotate(q_raw * inv_q * gain_query, cosine, sine).astype(BF16)
        query = query.reshape(length, kv_heads, heads // kv_heads, HEAD_DIM)
        key = rotate(k_raw * inv_k * gain_key, cosine, sine).astype(BF16)
        scores = jnp.where(allowed, mul("qjgd,kjd->jgqk", query, key) * scale, NEGATIVE)
        soft = jax.nn.softmax(scores, axis=-1)
        soft_low = soft.astype(BF16)
        mixed = mul("jgqk,kjd->qjgd", soft_low, value).astype(BF16).reshape(length, -1)
        resid = inputs + sum_scatter(mul("th,hd->td", mixed, wo), "seq")
        inv_post = inverse_root(resid)
        post = gather_rows((resid * inv_post * gain_post).astype(BF16))
        gate = mul("td,df->tf", post, wg)
        upper = mul("td,df->tf", post, wu)
        sigma = jax.nn.sigmoid(gate)
        hidden = (gate * sigma * upper).astype(BF16)
        outs.append((resid + sum_scatter(mul("tf,fd->td", hidden, wd), "seq")).astype(BF16))
        back_low = cotangent[at, 0]
        back = gather_rows(back_low)
        g_down = mul("tf,td->fd", hidden, back)
        d_hidden = mul("td,fd->tf", back, wd)
        d_gate = (d_hidden * upper * sigma * (1.0 + gate * (1.0 - sigma))).astype(BF16)
        d_upper = (d_hidden * gate * sigma).astype(BF16)
        g_gate = mul("td,tf->df", post, d_gate)
        g_up = mul("td,tf->df", post, d_upper)
        d_post = sum_scatter(mul("tf,df->td", d_gate, wg) + mul("tf,df->td", d_upper, wu), "seq")
        post_grad = jnp.sum(d_post * resid * inv_post, axis=0)
        d_resid = back_low.astype(F32) + norm_back(d_post, resid, inv_post, gain_post)
        d_attn = gather_rows(d_resid.astype(BF16))
        g_out = mul("th,td->hd", mixed, d_attn)
        d_mixed = mul("td,hd->th", d_attn, wo).astype(BF16)
        d_mixed = d_mixed.reshape(length, kv_heads, heads // kv_heads, HEAD_DIM)
        d_soft = mul("qjgd,kjd->jgqk", d_mixed, value)
        d_scores = (soft * (d_soft - jnp.sum(d_soft * soft, axis=-1, keepdims=True))).astype(BF16)
        d_query = mul("jgqk,kjd->qjgd", d_scores, key) * scale
        d_key = mul("jgqk,qjgd->kjd", d_scores, query) * scale
        d_value = mul("jgqk,qjgd->kjd", soft_low, d_mixed).astype(BF16).reshape(length, -1)
        key_turn = rotate_back(d_key, cosine, sine)
        query_turn = rotate_back(d_query.reshape(length, heads, HEAD_DIM), cosine, sine)
        key_grad = jnp.sum(key_turn * k_raw * inv_k, axis=(0, 1))
        query_grad = jnp.sum(query_turn * q_raw * inv_q, axis=(0, 1))
        d_key = norm_back(key_turn, k_raw, inv_k, gain_key).astype(BF16).reshape(length, -1)
        d_query = norm_back(query_turn, q_raw, inv_q, gain_query).astype(BF16).reshape(length, -1)
        g_query_w = mul("td,tf->df", normed, d_query)
        g_key_w = mul("td,tf->df", normed, d_key)
        g_value_w = mul("td,tf->df", normed, d_value)
        d_normed = mul("tf,df->td", d_query, wq) + mul("tf,df->td", d_key, wk)
        d_normed = sum_scatter(d_normed + mul("tf,df->td", d_value, wv), "seq")
        in_grad = jnp.sum(d_normed * inputs * inv_in, axis=0)
        token_grads.append(d_resid + norm_back(d_normed, inputs, inv_in, gain_in))
        found = [
            in_grad,
            post_grad,
            query_grad,
            key_grad,
            g_query_w,
            g_key_w,
            g_value_w,
            g_out,
            g_gate,
            g_up,
            g_down,
        ]
        grads = found if grads is None else [left + right for left, right in zip(grads, found)]
    small = [
        lax.psum_scatter(item, everyone, scatter_dimension=0, tiled=True) for item in grads[:4]
    ]

    def columns_home(item):
        full, wide = item.shape
        item = item.reshape(ways, -1, wide).astype(BF16)
        item = lax.psum_scatter(item, "fsdp", scatter_dimension=1, tiled=True)
        item = lax.all_to_all(item, "seq", 0, 0, tiled=True)
        return item.transpose(1, 0, 2).reshape(item.shape[1], ways * wide).astype(F32)

    def rows_home(item):
        return sum_scatter(item, "fsdp")

    large = [columns_home(item) for item in grads[4:7]] + [rows_home(grads[7])]
    large += [columns_home(item) for item in grads[8:10]] + [rows_home(grads[10])]
    return (jnp.stack(outs)[:, None], jnp.stack(token_grads)[:, None], *small, *large)


def solution(mesh):
    both = ("seq", "fsdp")
    act = P(None, "fsdp", "seq", None)
    vec, mat = (P(both), P(both, None))
    return jax.shard_map(
        plain_body,
        mesh=mesh,
        in_specs=(act, P(None, "fsdp", None), *[vec] * 4, *[mat] * 7, act),
        out_specs=(act, act, *[vec] * 4, *[mat] * 7),
        check_vma=False,
    )
```

profile of v0, /device:TPU:0, one launch (start us, length us, event | category | flops | bytes accessed | tf_op | source)
XLA Modules:
  0.0 1184.7 jit_solution(1742899532645338715)
XLA Ops:
  10.3 10.0 all_to_all.35
  22.3 40.7 %all-reduce.9 = (bf16[1024]{0:T(1024)(128)(2,1)S(1)}, bf16[128]{0:T(256)(128)(2,1)S(1)}, bf16[128]{0:T(256)(128)(2,1)S(1)}, bf16[1024]{0:T(1024)(128)(2,1)S(1)}) all-reduce(bf16[1024]{0:T(1024)(128)(2,1)S(1)} %dynamic-update-slice, bf16[128]{0:T(256)(128)(2,1)S(1)} %dynamic-update-slice.1, ...), channel_id=1, replica_groups=mesh['seq'=4,'fsdp'=8] {'seq','fsdp'}, use_global_device_ids=true, to_apply=%add | all-reduce | flops 2304 | bytes 9216
  77.7 17.0 %all-gather.27.cloned.1.call-done = bf16[1024,1024]{1,0:T(8,128)(2,1)} async-done(((bf16[256,1024]{1,0:T(8,128)(2,1)}), bf16[1024,1024]{1,0:T(8,128)(2,1)}) %all-gather.27.cloned.1.call-update) | async-done | bytes 2097168 | tf_op jit(solution)/shard_map/all_gather | solution.py:108
  98.6 20.2 %all-gather.15.cloned.1.call-done = bf16[1024,1024]{1,0:T(8,128)(2,1)} async-done(((bf16[256,1024]{1,0:T(8,128)(2,1)}), bf16[1024,1024]{1,0:T(8,128)(2,1)}) %all-gather.15.cloned.1.call-update) | async-done | bytes 2097168 | tf_op jit(solution)/shard_map/all_gather | solution.py:108
  128.4 4.6 multiply_reduce_fusion.1
  143.2 12.1 %fusion.168 = (f32[2,2,1024]{2,1,0:T(2,128)S(1)}, f32[2,2,1024,1024]{2,3,1,0:T(8,128)}) fusion(pred[1024,1024]{0,1:T(8,128)(4,1)} %broadcast_compare_fusion.1, bf16[1024,2,128,1]{0,2,3,1:T(8,128)(2,1)} %get-tuple-element.213, bf16[1024,2,2,128]{0,3,2,1:T(8,128)(2,1)} %get-tuple-element.184), kind=kOutput, calls=%fused_computation.314 | convolution fusion | flops 1090520064 | bytes 19415040 | tf_op jit(solution)/shard_map/sub | solution.py:127
  158.5 8.0 fusion.58
  166.5 4.2 convolution_convert_fusion.1
  175.6 11.8 fusion.169
  187.4 7.3 fusion.61
  199.8 9.8 all_to_all.36
  210.9 25.5 %reduce-scatter.20.cloned.1.call-done = bf16[256,1024]{1,0:T(8,128)(2,1)} async-done(((bf16[1024,1024]{1,0:T(8,128)(2,1)}), bf16[256,1024]{1,0:T(8,128)(2,1)}) %reduce-scatter.20.cloned.1.call-update) | async-done | bytes 524304 | tf_op jit(solution)/shard_map/reduce_scatter | solution.py:57
  243.0 56.6 %all-gather.23.cloned.1.call-done = bf16[4,256,1536]{2,0,1:T(4,128)(2,1)} async-done(((bf16[4,32,1536]{2,0,1:T(4,128)(2,1)}), bf16[4,256,1536]{2,0,1:T(4,128)(2,1)}) %all-gather.23.cloned.1.call-update) | async-done | bytes 3145744 | tf_op jit(solution)/shard_map/all_gather | solution.py:95
  299.6 4.2 copy.135
  303.8 18.6 %all-gather.29.cloned.1.call-done = bf16[1024,1024]{1,0:T(8,128)(2,1)} async-done(((bf16[256,1024]{1,0:T(8,128)(2,1)}), bf16[1024,1024]{1,0:T(8,128)(2,1)}) %all-gather.29.cloned.1.call-update) | async-done | bytes 2097168 | tf_op jit(solution)/shard_map/all_gather | solution.py:108
  322.4 5.6 fusion.120
  328.0 3.5 fusion.128
  331.5 37.3 %all-gather.25.cloned.1.call-done = bf16[768,1024]{1,0:T(8,128)(2,1)} async-done(((bf16[96,1024]{1,0:T(8,128)(2,1)}), bf16[768,1024]{1,0:T(8,128)(2,1)}) %all-gather.25.cloned.1.call-update) | async-done | bytes 1572880 | tf_op jit(solution)/shard_map/all_gather | solution.py:104
  368.8 22.8 %all-gather.37.cloned.1.call-done = bf16[1,1,1024,1024]{3,2,1,0:T(8,128)(2,1)} async-done(((bf16[1,1,256,1024]{3,2,1,0:T(8,128)(2,1)}), bf16[1,1,1024,1024]{3,2,1,0:T(8,128)(2,1)}) %all-gather.37.cloned.1.call-update) | async-done | bytes 2097168 | tf_op jit(solution)/shard_map/all_gather | solution.py:108
  391.7 8.0 multiply_convert_fusion
  405.2 10.6 all-gather.21.cloned.1.call-done
  415.9 5.6 fusion.122
  425.0 14.9 %all-gather.35.cloned.1.call-done = bf16[1,1,1024,1024]{3,2,1,0:T(8,128)(2,1)} async-done(((bf16[1,1,256,1024]{3,2,1,0:T(8,128)(2,1)}), bf16[1,1,1024,1024]{3,2,1,0:T(8,128)(2,1)}) %all-gather.35.cloned.1.call-update) | async-done | bytes 2097168 | tf_op jit(solution)/shard_map/all_gather | solution.py:108
  439.9 8.0 multiply_convert_fusion.2
  453.0 5.1 convolution_convert_fusion.2
  458.1 15.8 %reduce-scatter.28.cloned.1.call-done = bf16[256,1024]{1,0:T(8,128)(2,1)} async-done(((bf16[1024,1024]{1,0:T(8,128)(2,1)}), bf16[256,1024]{1,0:T(8,128)(2,1)}) %reduce-scatter.28.cloned.1.call-update) | async-done | bytes 524304 | tf_op jit(solution)/shard_map/reduce_scatter | solution.py:57
  473.9 34.0 %reduce-scatter.24.cloned.1.call-done = bf16[256,1024]{1,0:T(8,128)(2,1)} async-done(((bf16[1024,1024]{1,0:T(8,128)(2,1)}), bf16[256,1024]{1,0:T(8,128)(2,1)}) %reduce-scatter.24.cloned.1.call-update) | async-done | bytes 524304 | tf_op jit(solution)/shard_map/reduce_scatter | solution.py:57
  510.6 31.2 %reduce-scatter.22.cloned.1.call-done = bf16[256,1024]{1,0:T(8,128)(2,1)} async-done(((bf16[1024,1024]{1,0:T(8,128)(2,1)}), bf16[256,1024]{1,0:T(8,128)(2,1)}) %reduce-scatter.22.cloned.1.call-update) | async-done | bytes 524304 | tf_op jit(solution)/shard_map/reduce_scatter | solution.py:57
  546.0 4.1 fusion.175
  571.1 10.0 fusion.73
  581.2 8.2 fusion.5
  595.0 10.6 fusion.2
  605.6 12.2 %fusion.4 = bf16[2,2,1024,1024]{2,3,1,0:T(8,128)(2,1)S(1)} fusion(f32[2,1024,1024,2]{2,1,3,0:T(8,128)} %get-tuple-element.209, f32[2,2,1024]{2,1,0:T(2,128)S(1)} %get-tuple-element.208, f32[2,2,1024,1024]{2,3,1,0:T(8,128)} %get-tuple-element.203, f32[2,2,1024]{2,1,0:T(2,128)S(1)} %get-tuple-element.202), kind=kLoop, calls=%fused_computation.6 | loop fusion | flops 16777216 | bytes 41975808 | tf_op jit(solution)/shard_map/convert_element_type | solution.py:154
  625.0 12.7 %fusion.7 = bf16[2,2,1024,1024]{2,3,1,0:T(8,128)(2,1)S(1)} fusion(f32[2,1024,1024,2]{2,1,3,0:T(8,128)} %get-tuple-element.205, f32[2,2,1024]{2,1,0:T(2,128)S(1)} %get-tuple-element.204, f32[2,2,1024,1024]{2,3,1,0:T(8,128)} %get-tuple-element.201, f32[2,2,1024]{2,1,0:T(2,128)S(1)} %get-tuple-element.200), kind=kLoop, calls=%fused_computation.11 | loop fusion | flops 16777216 | bytes 41975808 | tf_op jit(solution)/shard_map/convert_element_type | solution.py:154
  649.0 8.9 fusion.70
  666.1 6.2 fusion.47
  695.9 4.5 convolution_convert_fusion.3
  703.9 24.1 %reduce-scatter.44.cloned.1.call-done = bf16[96,1024]{1,0:T(8,128)(2,1)} async-done(((bf16[768,1024]{1,0:T(8,128)(2,1)}), bf16[96,1024]{1,0:T(8,128)(2,1)}) %reduce-scatter.44.cloned.1.call-update) | async-done | bytes 196624 | tf_op jit(solution)/shard_map/reduce_scatter | solution.py:57
  729.6 65.8 %reduce-scatter.40.cloned.1.call-done = bf16[4,32,768]{2,1,0:T(8,128)(2,1)} async-done(((bf16[4,256,768]{2,1,0:T(8,128)(2,1)}), bf16[4,32,768]{2,1,0:T(8,128)(2,1)}) %reduce-scatter.40.cloned.1.call-update) | async-done | bytes 196624 | tf_op jit(solution)/shard_map/reduce_scatter | solution.py:192
  799.7 4.5 all-to-all-done.5
  805.0 55.2 %reduce-scatter.36.cloned.1.call-done = bf16[4,32,256]{2,1,0:T(8,128)(2,1)} async-done(((bf16[4,256,256]{2,1,0:T(8,128)(2,1)}), bf16[4,32,256]{2,1,0:T(8,128)(2,1)}) %reduce-scatter.36.cloned.1.call-update) | async-done | bytes 65552 | tf_op jit(solution)/shard_map/reduce_scatter | solution.py:192
  863.5 61.8 %reduce-scatter.34.cloned.1.call-done = bf16[4,32,256]{2,1,0:T(8,128)(2,1)} async-done(((bf16[4,256,256]{2,1,0:T(8,128)(2,1)}), bf16[4,32,256]{2,1,0:T(8,128)(2,1)}) %reduce-scatter.34.cloned.1.call-update) | async-done | bytes 65552 | tf_op jit(solution)/shard_map/reduce_scatter | solution.py:192
  928.6 4.1 all-to-all-done.3
  932.7 59.0 %reduce-scatter.32.cloned.1.call-done = bf16[4,32,512]{2,1,0:T(8,128)(2,1)} async-done(((bf16[4,256,512]{2,1,0:T(8,128)(2,1)}), bf16[4,32,512]{2,1,0:T(8,128)(2,1)}) %reduce-scatter.32.cloned.1.call-update) | async-done | bytes 131088 | tf_op jit(solution)/shard_map/reduce_scatter | solution.py:192
  996.4 61.8 %reduce-scatter.38.cloned.1.call-done = bf16[64,1024]{1,0:T(8,128)(2,1)} async-done(((bf16[512,1024]{1,0:T(8,128)(2,1)}), bf16[64,1024]{1,0:T(8,128)(2,1)}) %reduce-scatter.38.cloned.1.call-update) | async-done | bytes 131088 | tf_op jit(solution)/shard_map/reduce_scatter | solution.py:57
  1060.6 30.6 %reduce-scatter.30.cloned.1.call-done = bf16[256,1024]{1,0:T(8,128)(2,1)} async-done(((bf16[1024,1024]{1,0:T(8,128)(2,1)}), bf16[256,1024]{1,0:T(8,128)(2,1)}) %reduce-scatter.30.cloned.1.call-update) | async-done | bytes 524304 | tf_op jit(solution)/shard_map/reduce_scatter | solution.py:57
  1091.3 34.6 %reduce-scatter.26.cloned.1.call-done = bf16[256,1024]{1,0:T(8,128)(2,1)} async-done(((bf16[1024,1024]{1,0:T(8,128)(2,1)}), bf16[256,1024]{1,0:T(8,128)(2,1)}) %reduce-scatter.26.cloned.1.call-update) | async-done | bytes 524304 | tf_op jit(solution)/shard_map/reduce_scatter | solution.py:57
  1128.0 39.5 %all-reduce.8 = (f32[1024]{0:T(1024)S(1)}, f32[1024]{0:T(1024)S(1)}, f32[128]{0:T(128)S(1)}, f32[128]{0:T(128)S(1)}) all-reduce(f32[1024]{0:T(1024)S(1)} %add.287, f32[1024]{0:T(1024)S(1)} %add.288, f32[128]{0:T(128)S(1)} %add.289, f32[128]{0:T(128)S(1)} %add.290), channel_id=12, replica_groups=mesh['seq'=4,'fsdp'=8] {'seq','fsdp'}, use_global_device_ids=true, to_apply=%region_32.33.clone | all-reduce | flops 2304 | bytes 18432
  (503 shorter events, 196.6 us)
Async XLA Ops:
  7.2 68.2 %all-gather.17.cloned.1.call-start = ((), (), s32[]{:S(2)}) async-start(), calls=%async_computation.23 | async-start | bytes 2359296 | tf_op jit(solution)/shard_map/all_gather | solution.py:95
  21.3 73.3 %all-gather.27.cloned.1.call-start = ((), (), s32[]{:S(2)}) async-start(), calls=%async_computation.30 | async-start | bytes 2621440 | tf_op jit(solution)/shard_map/all_gather | solution.py:108
  65.8 53.0 %all-gather.15.cloned.1.call-start = ((), (), s32[]{:S(2)}) async-start(), calls=%async_computation.22 | async-start | bytes 2621440 | tf_op jit(solution)/shard_map/all_gather | solution.py:108
  66.6 99.9 %all-gather.19.cloned.1.call-start = ((), (), s32[]{:S(2)}) async-start(), calls=%async_computation.24 | async-start | bytes 1179648 | tf_op jit(solution)/shard_map/all_gather | solution.py:102
  67.1 143.7 %reduce-scatter.16.cloned.1.call-start = ((), (), s32[]{:S(2)}) async-start(), calls=%async_computation.25 | async-start | bytes 2621440 | tf_op jit(solution)/shard_map/reduce_scatter | solution.py:57
  170.7 65.6 %reduce-scatter.20.cloned.1.call-start = ((), (), s32[]{:S(2)}) async-start(), calls=%async_computation.31 | async-start | bytes 2621440 | tf_op jit(solution)/shard_map/reduce_scatter | solution.py:57
  198.4 101.2 %all-gather.23.cloned.1.call-start = ((), (), s32[]{:S(2)}) async-start(), calls=%async_computation.27 | async-start | bytes 3538944 | tf_op jit(solution)/shard_map/all_gather | solution.py:95
  210.7 111.7 %all-gather.29.cloned.1.call-start = ((), (), s32[]{:S(2)}) async-start(), calls=%async_computation.32 | async-start | bytes 2621440 | tf_op jit(solution)/shard_map/all_gather | solution.py:108
  210.8 330.9 %copy-start.75 = (f32[1024]{0:T(1024)}, f32[1024]{0:T(1024)S(1)}, u32[]{:S(2)}) copy-start(f32[1024]{0:T(1024)S(1)} %convert_element_type.312) | copy-start | bytes 12292
  238.1 303.7 %copy-start.87 = (f32[256]{0:T(256)}, f32[256]{0:T(256)S(1)}, u32[]{:S(2)}) copy-start(f32[256]{0:T(256)S(1)} %get-tuple-element.176) | copy-start | bytes 3076
  238.1 303.7 %copy-start.97 = (f32[256]{0:T(256)}, f32[256]{0:T(256)S(1)}, u32[]{:S(2)}) copy-start(f32[256]{0:T(256)S(1)} %get-tuple-element.175) | copy-start | bytes 3076
  238.1 303.6 %copy-start.89 = (f32[256]{0:T(256)}, f32[256]{0:T(256)S(1)}, u32[]{:S(2)}) copy-start(f32[256]{0:T(256)S(1)} %get-tuple-element.178) | copy-start | bytes 3076
  238.1 303.6 %copy-start.101 = (f32[256]{0:T(256)}, f32[256]{0:T(256)S(1)}, u32[]{:S(2)}) copy-start(f32[256]{0:T(256)S(1)} %get-tuple-element.177) | copy-start | bytes 3076
  239.5 129.3 %all-gather.25.cloned.1.call-start = ((), (), s32[]{:S(2)}) async-start(), calls=%async_computation.28 | async-start | bytes 1769472 | tf_op jit(solution)/shard_map/all_gather | solution.py:104
  240.2 151.4 %all-gather.37.cloned.1.call-start = ((), (), s32[]{:S(2)}) async-start(), calls=%async_computation.48 | async-start | bytes 2621440 | tf_op jit(solution)/shard_map/all_gather | solution.py:108
  241.4 174.4 %all-gather.21.cloned.1.call-start = ((), (), s32[]{:S(2)}) async-start(), calls=%async_computation.26 | async-start | bytes 2621440 | tf_op jit(solution)/shard_map/all_gather | solution.py:108
  242.2 197.7 %all-gather.35.cloned.1.call-start = ((), (), s32[]{:S(2)}) async-start(), calls=%async_computation.47 | async-start | bytes 2621440 | tf_op jit(solution)/shard_map/all_gather | solution.py:108
  242.7 231.1 %reduce-scatter.28.cloned.1.call-start = ((), (), s32[]{:S(2)}) async-start(), calls=%async_computation.37 | async-start | bytes 2621440 | tf_op jit(solution)/shard_map/reduce_scatter | solution.py:57
  404.8 103.1 %reduce-scatter.24.cloned.1.call-start = ((), (), s32[]{:S(2)}) async-start(), calls=%async_computation.34 | async-start | bytes 2621440 | tf_op jit(solution)/shard_map/reduce_scatter | solution.py:57
  452.9 88.8 %reduce-scatter.22.cloned.1.call-start = ((), (), s32[]{:S(2)}) async-start(), calls=%async_computation.33 | async-start | bytes 2621440 | tf_op jit(solution)/shard_map/reduce_scatter | solution.py:57
  458.1 109.9 %all-gather.31.cloned.1.call-start = ((), (), s32[]{:S(2)}) async-start(), calls=%async_computation.35 | async-start | bytes 2621440 | tf_op jit(solution)/shard_map/all_gather | solution.py:108
  545.2 46.9 %all-gather.33.cloned.1.call-start = ((), (), s32[]{:S(2)}) async-start(), calls=%async_computation.38 | async-start | bytes 2621440 | tf_op jit(solution)/shard_map/all_gather | solution.py:108
  545.8 154.7 %reduce-scatter.42.cloned.1.call-start = ((), (), s32[]{:S(2)}) async-start(), calls=%async_computation.45 | async-start | bytes 1769472 | tf_op jit(solution)/shard_map/reduce_scatter | solution.py:192
  553.4 174.5 %reduce-scatter.44.cloned.1.call-start = ((), (), s32[]{:S(2)}) async-start(), calls=%async_computation.46 | async-start | bytes 1769472 | tf_op jit(solution)/shard_map/reduce_scatter | solution.py:57
  560.1 235.4 %reduce-scatter.40.cloned.1.call-start = ((), (), s32[]{:S(2)}) async-start(), calls=%async_computation.44 | async-start | bytes 1769472 | tf_op jit(solution)/shard_map/reduce_scatter | solution.py:192
  566.9 293.3 %reduce-scatter.36.cloned.1.call-start = ((), (), s32[]{:S(2)}) async-start(), calls=%async_computation.42 | async-start | bytes 589824 | tf_op jit(solution)/shard_map/reduce_scatter | solution.py:192
  659.5 265.8 %reduce-scatter.34.cloned.1.call-start = ((), (), s32[]{:S(2)}) async-start(), calls=%async_computation.41 | async-start | bytes 589824 | tf_op jit(solution)/shard_map/reduce_scatter | solution.py:192
  665.7 326.0 %reduce-scatter.32.cloned.1.call-start = ((), (), s32[]{:S(2)}) async-start(), calls=%async_computation.40 | async-start | bytes 1179648 | tf_op jit(solution)/shard_map/reduce_scatter | solution.py:192
  679.5 378.8 %reduce-scatter.38.cloned.1.call-start = ((), (), s32[]{:S(2)}) async-start(), calls=%async_computation.43 | async-start | bytes 1179648 | tf_op jit(solution)/shard_map/reduce_scatter | solution.py:57
  683.7 407.6 %reduce-scatter.30.cloned.1.call-start = ((), (), s32[]{:S(2)}) async-start(), calls=%async_computation.39 | async-start | bytes 2621440 | tf_op jit(solution)/shard_map/reduce_scatter | solution.py:57
  688.8 437.1 %reduce-scatter.26.cloned.1.call-start = ((), (), s32[]{:S(2)}) async-start(), calls=%async_computation.36 | async-start | bytes 2621440 | tf_op jit(solution)/shard_map/reduce_scatter | solution.py:57
  694.5 478.3 %reduce-scatter.18.cloned.1.call-start = ((), (), s32[]{:S(2)}) async-start(), calls=%async_computation.29 | async-start | bytes 2621440 | tf_op jit(solution)/shard_map/reduce_scatter | solution.py:57
  700.5 95.0 %all-to-all-start.6 = ((bf16[4,32,768]{2,1,0:T(8,128)(2,1)}), bf16[4,32,768]{2,1,0:T(8,128)(2,1)S(1)}, u32[]{:S(2)}, u32[]{:S(2)}) async-start(bf16[4,32,768]{2,1,0:T(8,128)(2,1)} %reduce-scatter.42.cloned.1.call-done), calls=%async_computation.20 | async-start | bytes 393216 | tf_op jit(solution)/shard_map/all_to_all | solution.py:193
  795.5 8.7 all-to-all-start.5
  799.7 326.2 %copy-start.1 = (bf16[2,1,256,1024]{3,2,1,0:T(8,128)(2,1)S(1)}, bf16[2,1,256,1024]{3,2,1,0:T(8,128)(2,1)}, u32[]{:S(2)}) copy-start(bf16[2,1,256,1024]{3,2,1,0:T(8,128)(2,1)} %param.14) | copy-start | bytes 3145732
  799.7 326.2 %copy-start.82 = (f32[1024]{0:T(1024)S(1)}, f32[1024]{0:T(1024)}, u32[]{:S(2)}) copy-start(f32[1024]{0:T(1024)} %copy-done.81) | copy-start | bytes 12292
  799.7 326.2 %copy-start.92 = (f32[256]{0:T(256)S(1)}, f32[256]{0:T(256)}, u32[]{:S(2)}) copy-start(f32[256]{0:T(256)} %copy-done.91) | copy-start | bytes 3076
  799.7 326.2 %copy-start.96 = (f32[256]{0:T(256)S(1)}, f32[256]{0:T(256)}, u32[]{:S(2)}) copy-start(f32[256]{0:T(256)} %copy-done.95) | copy-start | bytes 3076
  860.2 65.1 %all-to-all-start.4 = ((bf16[4,32,256]{2,1,0:T(8,128)(2,1)}), bf16[4,32,256]{2,1,0:T(8,128)(2,1)S(1)}, u32[]{:S(2)}, u32[]{:S(2)}) async-start(bf16[4,32,256]{2,1,0:T(8,128)(2,1)} %reduce-scatter.36.cloned.1.call-done), calls=%async_computation.15 | async-start | bytes 131072 | tf_op jit(solution)/shard_map/all_to_all | solution.py:193
  925.3 7.4 all-to-all-start.3
  991.7 68.2 %all-to-all-start.2 = ((bf16[4,32,512]{2,1,0:T(8,128)(2,1)}), bf16[4,32,512]{2,1,0:T(8,128)(2,1)S(1)}, u32[]{:S(2)}, u32[]{:S(2)}) async-start(bf16[4,32,512]{2,1,0:T(8,128)(2,1)} %reduce-scatter.32.cloned.1.call-done), calls=%async_computation.11 | async-start | bytes 262144 | tf_op jit(solution)/shard_map/all_to_all | solution.py:193
  995.0 174.8 %copy-start.27 = (bf16[256,1024]{1,0:T(8,128)(2,1)S(1)}, bf16[256,1024]{1,0:T(8,128)(2,1)}, u32[]{:S(2)}) copy-start(bf16[256,1024]{1,0:T(8,128)(2,1)} %reduce-scatter.20.cloned.1.call-done) | copy-start | bytes 1572868
  995.0 174.8 %copy-start.33 = (bf16[2,1,256,1024]{3,2,1,0:T(8,128)(2,1)S(1)}, bf16[2,1,256,1024]{3,2,1,0:T(8,128)(2,1)}, u32[]{:S(2)}) copy-start(bf16[2,1,256,1024]{3,2,1,0:T(8,128)(2,1)} %param.27) | copy-start | bytes 3145732
  995.0 174.8 %copy-start.76 = (f32[1024]{0:T(1024)S(1)}, f32[1024]{0:T(1024)}, u32[]{:S(2)}) copy-start(f32[1024]{0:T(1024)} %copy-done.75) | copy-start | bytes 12292
  995.0 174.8 %copy-start.90 = (f32[256]{0:T(256)S(1)}, f32[256]{0:T(256)}, u32[]{:S(2)}) copy-start(f32[256]{0:T(256)} %copy-done.89) | copy-start | bytes 3076
  995.0 174.8 %copy-start.102 = (f32[256]{0:T(256)S(1)}, f32[256]{0:T(256)}, u32[]{:S(2)}) copy-start(f32[256]{0:T(256)} %copy-done.101) | copy-start | bytes 3076
  995.0 174.8 %copy-start.104 = (f32[256]{0:T(256)S(1)}, f32[256]{0:T(256)}, u32[]{:S(2)}) copy-start(f32[256]{0:T(256)} %copy-done.103) | copy-start | bytes 3076
  995.1 174.8 %copy-start.109 = (f32[256]{0:T(256)S(1)}, f32[256]{0:T(256)}, u32[]{:S(2)}) copy-start(f32[256]{0:T(256)} %get-tuple-element.173) | copy-start | bytes 3076
  (130 other events, 1143.4 us)
Sparse Core Ops, SparseCore 0:
  21.4 50.4 all-gather.16
  73.5 21.0 all-gather.26
  96.2 22.5 all-gather.14
  120.8 40.1 all-gather.18
  170.9 31.4 reduce-scatter.15
  204.9 31.4 reduce-scatter.19
  239.1 60.4 all-gather.22
  301.2 21.1 all-gather.28
  324.6 44.1 all-gather.24
  370.2 21.3 all-gather.36
  393.2 22.5 all-gather.20
  417.3 22.5 all-gather.34
  442.4 31.4 reduce-scatter.27
  476.4 31.4 reduce-scatter.23
  510.3 31.4 reduce-scatter.21
  545.3 22.6 all-gather.30
  569.5 22.5 all-gather.32
  595.8 64.8 reduce-scatter.41
  664.1 63.7 reduce-scatter.43
  731.6 63.8 reduce-scatter.39
  798.8 61.2 reduce-scatter.35
  863.9 61.3 reduce-scatter.33
  928.7 62.8 reduce-scatter.31
  995.9 62.3 reduce-scatter.37
  1060.8 30.4 reduce-scatter.29
  1094.4 31.4 reduce-scatter.25
  1128.2 31.5 reduce-scatter.17
where the time goes:
time: 1190 us; the launch traced here: 1180 us
  waiting for transfers between devices  714 us (60%)
  matrix products  210 us (18%)
  blocking collectives  100 us (8%)
  other arithmetic  88.6 us (7%)
  local copies, waits for them, and re-layouts  36.6 us (3%)
  starting transfers between devices  19.4 us (2%)
  between operations  16.5 us (1%)
    reduce_scatter x10, waiting for transfers between devices, sum_scatter(): lax.psum_scatter(part.astype(BF16), axis, scatter_dimension=0, tiled=True)  258 us
    reduce_scatter x5, waiting for transfers between devices, columns_home(): item = lax.psum_scatter(item, 'fsdp', scatter_dimension=1, tiled=True)  242 us
    dot_general x52, matrix products, mul(): return jnp.einsum(eq, left, right, preferred_element_type=F32)  186 us
    all_gather x8, waiting for transfers between devices, gather_rows(): return lax.all_gather(item, 'seq', axis=0, tiled=True)  108 us
    unnamed x2, blocking collectives  80.2 us
    all_gather x2, waiting for transfers between devices, spread(): packed = lax.all_gather(packed, 'fsdp', axis=1, tiled=True)  56.6 us
    all_gather x1, waiting for transfers between devices, plain_body(): wd = lax.all_gather(w_down, 'fsdp', axis=0, tiled=True)  37.3 us
    convert_element_type x2, other arithmetic, plain_body(): (soft * (d_soft - jnp.sum(d_soft * soft, axis=-1, keepdims=True))).astype...  24.9 us
  transfers between devices with their start and end apart: 32, of which 24 were waited for; matrix products, arithmetic and copies ran while one was open for 25% of the time, Pallas kernels for 0%

commit v1 on v0

--- a/solution.py
+++ b/solution.py
@@ -92,7 +92,14 @@
     def spread(*items):
         packed = jnp.concatenate([slice_weights(item, ways) for item in items], axis=2)
         packed = lax.all_to_all(packed, "seq", 0, 0, tiled=True)
-        packed = lax.all_gather(packed, "fsdp", axis=1, tiled=True)
+        ring = [packed]
+        for hop in range(7):
+            ring.append(lax.ppermute(ring[-1], "fsdp", [(dev, (dev + 1) % 8) for dev in range(8)]))
+        packed = jnp.roll(
+            jnp.concatenate(ring[::-1], axis=1),
+            (lax.axis_index("fsdp") + 1) * ring[0].shape[1],
+            axis=1,
+        )
         packed = packed.reshape(-1, packed.shape[2])
         sizes = [item.shape[1] // ways for item in items]
         cuts = [sum(sizes[: at + 1]) for at in range(len(sizes) - 1)]

time: 1190 us -> 1160 us (0.975)
  waiting for transfers between devices: 714 us -> 679 us
    ppermute x0 -> x14, waiting for transfers between devices: none -> 159 us  [spread(): lax.ppermute(ring[-1], 'fsdp', [(dev, (dev + 1) % 8) for dev in range(8)])]
    all_gather x8, waiting for transfers between devices: 108 us -> 5.28 us  [gather_rows(): return lax.all_gather(item, 'seq', axis=0, tiled=True)]
    all_gather x2 -> x0, waiting for transfers between devices: 56.6 us -> none  [spread(): packed = lax.all_gather(packed, 'fsdp', axis=1, tiled=True)]
    all_gather x1, waiting for transfers between devices: 37.3 us -> 0.01 us  [plain_body(): wd = lax.all_gather(w_down, 'fsdp', axis=0, tiled=True)]
    unnamed x304 -> x348, local copies, waits for them, and re-layouts: 20.3 us -> 33.2 us
  transfers between devices with their start and end apart: 32 -> 44, of which waited for: 24 -> 31; matrix products, arithmetic and copies ran while one was open for 25% -> 25% of each run, Pallas kernels for 0% -> 0%
where the time goes in v1:
time: 1160 us; the launch traced here: 1150 us
  waiting for transfers between devices  679 us (59%)
  matrix products  203 us (18%)
  blocking collectives  102 us (9%)
  other arithmetic  87.9 us (8%)
  local copies, waits for them, and re-layouts  43.7 us (4%)
  starting transfers between devices  22.1 us (2%)
  between operations  16.6 us (1%)
    reduce_scatter x10, waiting for transfers between devices, sum_scatter(): lax.psum_scatter(part.astype(BF16), axis, scatter_dimension=0, tiled=True)  262 us
    reduce_scatter x5, waiting for transfers between devices, columns_home(): item = lax.psum_scatter(item, 'fsdp', scatter_dimension=1, tiled=True)  242 us
    dot_general x52, matrix products, mul(): return jnp.einsum(eq, left, right, preferred_element_type=F32)  180 us
    ppermute x14, waiting for transfers between devices, spread(): lax.ppermute(ring[-1], 'fsdp', [(dev, (dev + 1) % 8) for dev in range(8)])  159 us
    unnamed x2, blocking collectives  81.7 us
    unnamed x348, local copies, waits for them, and re-layouts  33.2 us
    convert_element_type x2, other arithmetic, plain_body(): (soft * (d_soft - jnp.sum(d_soft * soft, axis=-1, keepdims=True))).astype...  24.9 us
    sub x2, matrix products, plain_body(): soft = jax.nn.softmax(scores, axis=-1)  23.6 us
  transfers between devices with their start and end apart: 44, of which 31 were waited for; matrix products, arithmetic and copies ran while one was open for 25% of the time, Pallas kernels for 0%

profile of v1, /device:TPU:0, one launch (start us, length us, event | category | flops | bytes accessed | tf_op | source)
XLA Modules:
  0.0 1154.6 jit_solution(9627285327248679021)
XLA Ops:
  10.6 42.1 %all-reduce.9 = (bf16[1024]{0:T(1024)(128)(2,1)S(1)}, bf16[128]{0:T(256)(128)(2,1)S(1)}, bf16[128]{0:T(256)(128)(2,1)S(1)}, bf16[1024]{0:T(1024)(128)(2,1)S(1)}) all-reduce(bf16[1024]{0:T(1024)(128)(2,1)S(1)} %dynamic-update-slice, bf16[128]{0:T(256)(128)(2,1)S(1)} %dynamic-update-slice.1, ...), channel_id=1, replica_groups=mesh['seq'=4,'fsdp'=8] {'seq','fsdp'}, use_global_device_ids=true, to_apply=%add | all-reduce | flops 2304 | bytes 9216
  59.1 10.5 all_to_all.35
  70.8 8.8 collective-permute-done
  79.6 9.1 collective-permute-done.1
  88.9 9.0 collective-permute-done.2
  99.8 7.1 collective-permute-done.3
  108.8 7.9 collective-permute-done.4
  118.9 11.7 %collective-permute-done.5 = bf16[4,32,1024]{2,1,0:T(8,128)(2,1)S(1)} collective-permute-done((bf16[4,32,1024]{2,1,0:T(8,128)(2,1)S(1)}, bf16[4,32,1024]{2,1,0:T(8,128)(2,1)S(1)}, u32[]{:S(2)}, u32[]{:S(2)}) %collective-permute-start.5) | collective-permute-done | bytes 262176 | tf_op jit(solution)/shard_map/ppermute | solution.py:97
  132.6 11.9 %collective-permute-done.6 = bf16[4,32,1024]{2,1,0:T(8,128)(2,1)S(1)} collective-permute-done((bf16[4,32,1024]{2,1,0:T(8,128)(2,1)S(1)}, bf16[4,32,1024]{2,1,0:T(8,128)(2,1)S(1)}, u32[]{:S(2)}, u32[]{:S(2)}) %collective-permute-start.6) | collective-permute-done | bytes 262176 | tf_op jit(solution)/shard_map/ppermute | solution.py:97
  150.3 4.5 multiply_reduce_fusion
  170.0 12.1 %fusion.169 = (f32[2,2,1024]{2,1,0:T(2,128)S(1)}, f32[2,2,1024,1024]{2,3,1,0:T(8,128)}) fusion(pred[1024,1024]{0,1:T(8,128)(4,1)} %broadcast_compare_fusion, bf16[1024,2,128,1]{0,2,3,1:T(8,128)(2,1)} %get-tuple-element.212, bf16[1024,2,2,128]{0,3,2,1:T(8,128)(2,1)} %get-tuple-element.185), kind=kOutput, calls=%fused_computation.349 | convolution fusion | flops 1090520064 | bytes 19415040 | tf_op jit(solution)/shard_map/sub | solution.py:134
  185.3 7.1 fusion.61
  201.5 11.5 fusion.168
  213.0 7.4 fusion.58
  226.7 31.4 %reduce-scatter.16.cloned.1.call-done = bf16[256,1024]{1,0:T(8,128)(2,1)} async-done(((bf16[1024,1024]{1,0:T(8,128)(2,1)}), bf16[256,1024]{1,0:T(8,128)(2,1)}) %reduce-scatter.16.cloned.1.call-update) | async-done | bytes 524304 | tf_op jit(solution)/shard_map/reduce_scatter | solution.py:57
  262.1 9.8 all_to_all.36
  273.4 15.5 %collective-permute-done.7 = bf16[4,32,1536]{2,1,0:T(8,128)(2,1)S(1)} collective-permute-done((bf16[4,32,1536]{2,1,0:T(8,128)(2,1)S(1)}, bf16[4,32,1536]{2,1,0:T(8,128)(2,1)S(1)}, u32[]{:S(2)}, u32[]{:S(2)}) %collective-permute-start.7) | collective-permute-done | bytes 393248 | tf_op jit(solution)/shard_map/ppermute | solution.py:97
  289.7 20.5 %collective-permute-done.8 = bf16[4,32,1536]{2,1,0:T(8,128)(2,1)S(1)} collective-permute-done((bf16[4,32,1536]{2,1,0:T(8,128)(2,1)S(1)}, bf16[4,32,1536]{2,1,0:T(8,128)(2,1)S(1)}, u32[]{:S(2)}, u32[]{:S(2)}) %collective-permute-start.8) | collective-permute-done | bytes 393248 | tf_op jit(solution)/shard_map/ppermute | solution.py:97
  311.0 13.0 %collective-permute-done.9 = bf16[4,32,1536]{2,1,0:T(8,128)(2,1)S(1)} collective-permute-done((bf16[4,32,1536]{2,1,0:T(8,128)(2,1)S(1)}, bf16[4,32,1536]{2,1,0:T(8,128)(2,1)S(1)}, u32[]{:S(2)}, u32[]{:S(2)}) %collective-permute-start.9) | collective-permute-done | bytes 393248 | tf_op jit(solution)/shard_map/ppermute | solution.py:97
  324.7 12.1 %collective-permute-done.10 = bf16[4,32,1536]{2,1,0:T(8,128)(2,1)S(1)} collective-permute-done((bf16[4,32,1536]{2,1,0:T(8,128)(2,1)S(1)}, bf16[4,32,1536]{2,1,0:T(8,128)(2,1)S(1)}, u32[]{:S(2)}, u32[]{:S(2)}) %collective-permute-start.10) | collective-permute-done | bytes 393248 | tf_op jit(solution)/shard_map/ppermute | solution.py:97
  337.6 11.2 collective-permute-done.11
  349.5 10.6 collective-permute-done.12
  360.2 10.7 collective-permute-done.13
  383.2 5.5 fusion.42
  393.3 4.7 multiply_convert_fusion
  403.5 5.5 fusion.50
  415.4 4.8 multiply_convert_fusion.2
  425.3 5.0 convolution_convert_fusion.2
  430.4 14.4 %reduce-scatter.28.cloned.1.call-done = bf16[256,1024]{1,0:T(8,128)(2,1)} async-done(((bf16[1024,1024]{1,0:T(8,128)(2,1)}), bf16[256,1024]{1,0:T(8,128)(2,1)}) %reduce-scatter.28.cloned.1.call-update) | async-done | bytes 524304 | tf_op jit(solution)/shard_map/reduce_scatter | solution.py:57
  444.8 34.0 %reduce-scatter.24.cloned.1.call-done = bf16[256,1024]{1,0:T(8,128)(2,1)} async-done(((bf16[1024,1024]{1,0:T(8,128)(2,1)}), bf16[256,1024]{1,0:T(8,128)(2,1)}) %reduce-scatter.24.cloned.1.call-update) | async-done | bytes 524304 | tf_op jit(solution)/shard_map/reduce_scatter | solution.py:57
  481.4 31.3 %reduce-scatter.22.cloned.1.call-done = bf16[256,1024]{1,0:T(8,128)(2,1)} async-done(((bf16[1024,1024]{1,0:T(8,128)(2,1)}), bf16[256,1024]{1,0:T(8,128)(2,1)}) %reduce-scatter.22.cloned.1.call-update) | async-done | bytes 524304 | tf_op jit(solution)/shard_map/reduce_scatter | solution.py:57
  542.0 10.0 fusion.73
  552.1 8.2 fusion.5
  565.9 10.6 fusion.2
  576.5 12.3 %fusion.4 = bf16[2,2,1024,1024]{2,3,1,0:T(8,128)(2,1)S(1)} fusion(f32[2,1024,1024,2]{2,1,3,0:T(8,128)} %get-tuple-element.209, f32[2,2,1024]{2,1,0:T(2,128)S(1)} %get-tuple-element.208, f32[2,2,1024,1024]{2,3,1,0:T(8,128)} %get-tuple-element.203, f32[2,2,1024]{2,1,0:T(2,128)S(1)} %copy-done.97), kind=kLoop, calls=%fused_computation.6 | loop fusion | flops 16777216 | bytes 41975808 | tf_op jit(solution)/shard_map/convert_element_type | solution.py:161
  593.2 12.7 %fusion.7 = bf16[2,2,1024,1024]{2,3,1,0:T(8,128)(2,1)S(1)} fusion(f32[2,1024,1024,2]{2,1,3,0:T(8,128)} %get-tuple-element.205, f32[2,2,1024]{2,1,0:T(2,128)S(1)} %get-tuple-element.204, f32[2,2,1024,1024]{2,3,1,0:T(8,128)} %get-tuple-element.201, f32[2,2,1024]{2,1,0:T(2,128)S(1)} %copy-done.99), kind=kLoop, calls=%fused_computation.11 | loop fusion | flops 16777216 | bytes 41975808 | tf_op jit(solution)/shard_map/convert_element_type | solution.py:161
  619.4 8.9 fusion.70
  636.4 6.2 fusion.47
  666.3 4.5 convolution_convert_fusion.3
  674.3 24.5 %reduce-scatter.44.cloned.1.call-done = bf16[96,1024]{1,0:T(8,128)(2,1)} async-done(((bf16[768,1024]{1,0:T(8,128)(2,1)}), bf16[96,1024]{1,0:T(8,128)(2,1)}) %reduce-scatter.44.cloned.1.call-update) | async-done | bytes 196624 | tf_op jit(solution)/shard_map/reduce_scatter | solution.py:57
  700.5 65.8 %reduce-scatter.40.cloned.1.call-done = bf16[4,32,768]{2,1,0:T(8,128)(2,1)} async-done(((bf16[4,256,768]{2,1,0:T(8,128)(2,1)}), bf16[4,32,768]{2,1,0:T(8,128)(2,1)}) %reduce-scatter.40.cloned.1.call-update) | async-done | bytes 196624 | tf_op jit(solution)/shard_map/reduce_scatter | solution.py:199
  775.8 55.1 %reduce-scatter.36.cloned.1.call-done = bf16[4,32,256]{2,1,0:T(8,128)(2,1)} async-done(((bf16[4,256,256]{2,1,0:T(8,128)(2,1)}), bf16[4,32,256]{2,1,0:T(8,128)(2,1)}) %reduce-scatter.36.cloned.1.call-update) | async-done | bytes 65552 | tf_op jit(solution)/shard_map/reduce_scatter | solution.py:199
  834.2 61.6 %reduce-scatter.34.cloned.1.call-done = bf16[4,32,256]{2,1,0:T(8,128)(2,1)} async-done(((bf16[4,256,256]{2,1,0:T(8,128)(2,1)}), bf16[4,32,256]{2,1,0:T(8,128)(2,1)}) %reduce-scatter.34.cloned.1.call-update) | async-done | bytes 65552 | tf_op jit(solution)/shard_map/reduce_scatter | solution.py:199
  903.2 59.0 %reduce-scatter.32.cloned.1.call-done = bf16[4,32,512]{2,1,0:T(8,128)(2,1)} async-done(((bf16[4,256,512]{2,1,0:T(8,128)(2,1)}), bf16[4,32,512]{2,1,0:T(8,128)(2,1)}) %reduce-scatter.32.cloned.1.call-update) | async-done | bytes 131088 | tf_op jit(solution)/shard_map/reduce_scatter | solution.py:199
  966.9 61.6 %reduce-scatter.38.cloned.1.call-done = bf16[64,1024]{1,0:T(8,128)(2,1)} async-done(((bf16[512,1024]{1,0:T(8,128)(2,1)}), bf16[64,1024]{1,0:T(8,128)(2,1)}) %reduce-scatter.38.cloned.1.call-update) | async-done | bytes 131088 | tf_op jit(solution)/shard_map/reduce_scatter | solution.py:57
  1030.9 30.6 %reduce-scatter.30.cloned.1.call-done = bf16[256,1024]{1,0:T(8,128)(2,1)} async-done(((bf16[1024,1024]{1,0:T(8,128)(2,1)}), bf16[256,1024]{1,0:T(8,128)(2,1)}) %reduce-scatter.30.cloned.1.call-update) | async-done | bytes 524304 | tf_op jit(solution)/shard_map/reduce_scatter | solution.py:57
  1061.5 34.6 %reduce-scatter.26.cloned.1.call-done = bf16[256,1024]{1,0:T(8,128)(2,1)} async-done(((bf16[1024,1024]{1,0:T(8,128)(2,1)}), bf16[256,1024]{1,0:T(8,128)(2,1)}) %reduce-scatter.26.cloned.1.call-update) | async-done | bytes 524304 | tf_op jit(solution)/shard_map/reduce_scatter | solution.py:57
  1098.2 39.6 %all-reduce.8 = (f32[1024]{0:T(1024)S(1)}, f32[1024]{0:T(1024)S(1)}, f32[128]{0:T(128)S(1)}, f32[128]{0:T(128)S(1)}) all-reduce(f32[1024]{0:T(1024)S(1)} %add.308, f32[1024]{0:T(1024)S(1)} %add.309, f32[128]{0:T(128)S(1)} %add.310, f32[128]{0:T(128)S(1)} %add.311), channel_id=12, replica_groups=mesh['seq'=4,'fsdp'=8] {'seq','fsdp'}, use_global_device_ids=true, to_apply=%region_32.33.clone | all-reduce | flops 2304 | bytes 18432
  (569 shorter events, 231.6 us)
Async XLA Ops:
  7.2 139.3 %all-gather.13.cloned.1.call-start = ((), (), s32[]{:S(2)}) async-start(), calls=%async_computation.22 | async-start | bytes 2621440 | tf_op jit(solution)/shard_map/all_gather | solution.py:115
  57.9 92.4 %all-gather.21.cloned.1.call-start = ((), (), s32[]{:S(2)}) async-start(), calls=%async_computation.28 | async-start | bytes 2621440 | tf_op jit(solution)/shard_map/all_gather | solution.py:115
  58.6 133.8 %all-gather.15.cloned.1.call-start = ((), (), s32[]{:S(2)}) async-start(), calls=%async_computation.23 | async-start | bytes 1179648 | tf_op jit(solution)/shard_map/all_gather | solution.py:109
  69.6 10.1 collective-permute-start
  79.6 9.2 collective-permute-start.1
  88.8 9.1 collective-permute-start.2
  88.8 137.8 %reduce-scatter.20.cloned.1.call-start = ((), (), s32[]{:S(2)}) async-start(), calls=%async_computation.29 | async-start | bytes 2621440 | tf_op jit(solution)/shard_map/reduce_scatter | solution.py:57
  97.8 9.1 collective-permute-start.3
  106.9 9.8 collective-permute-start.4
  116.8 13.9 %collective-permute-start.5 = (bf16[4,32,1024]{2,1,0:T(8,128)(2,1)S(1)}, bf16[4,32,1024]{2,1,0:T(8,128)(2,1)S(1)}, u32[]{:S(2)}, u32[]{:S(2)}) collective-permute-start(bf16[4,32,1024]{2,1,0:T(8,128)(2,1)S(1)} %collective-permute-done.4), channel_id=1, source_target_pairs={{0,1},{1,2},{2,3},{3,4},{4,5},{5,6},{6,7},{7,0},{8,9},{9,10},{10,1... | collective-permute-start | bytes 786440 | tf_op jit(solution)/shard_map/ppermute | solution.py:97
  130.7 13.9 %collective-permute-start.6 = (bf16[4,32,1024]{2,1,0:T(8,128)(2,1)S(1)}, bf16[4,32,1024]{2,1,0:T(8,128)(2,1)S(1)}, u32[]{:S(2)}, u32[]{:S(2)}) collective-permute-start(bf16[4,32,1024]{2,1,0:T(8,128)(2,1)S(1)} %collective-permute-done.5), channel_id=1, source_target_pairs={{0,1},{1,2},{2,3},{3,4},{4,5},{5,6},{6,7},{7,0},{8,9},{9,10},{10,1... | collective-permute-start | bytes 786440 | tf_op jit(solution)/shard_map/ppermute | solution.py:97
  196.6 61.4 %reduce-scatter.16.cloned.1.call-start = ((), (), s32[]{:S(2)}) async-start(), calls=%async_computation.24 | async-start | bytes 2621440 | tf_op jit(solution)/shard_map/reduce_scatter | solution.py:57
  224.0 159.1 %all-gather.19.cloned.1.call-start = ((), (), s32[]{:S(2)}) async-start(), calls=%async_computation.26 | async-start | bytes 1769472 | tf_op jit(solution)/shard_map/all_gather | solution.py:111
  224.6 158.6 %all-gather.31.cloned.1.call-start = ((), (), s32[]{:S(2)}) async-start(), calls=%async_computation.46 | async-start | bytes 2621440 | tf_op jit(solution)/shard_map/all_gather | solution.py:115
  226.3 162.4 %all-gather.23.cloned.1.call-start = ((), (), s32[]{:S(2)}) async-start(), calls=%async_computation.30 | async-start | bytes 2621440 | tf_op jit(solution)/shard_map/all_gather | solution.py:115
  261.8 141.7 %all-gather.29.cloned.1.call-start = ((), (), s32[]{:S(2)}) async-start(), calls=%async_computation.45 | async-start | bytes 2621440 | tf_op jit(solution)/shard_map/all_gather | solution.py:115
  271.9 17.0 %collective-permute-start.7 = (bf16[4,32,1536]{2,1,0:T(8,128)(2,1)S(1)}, bf16[4,32,1536]{2,1,0:T(8,128)(2,1)S(1)}, u32[]{:S(2)}, u32[]{:S(2)}) collective-permute-start(bf16[4,32,1536]{2,1,0:T(8,128)(2,1)S(1)} %all_to_all.36), channel_id=1, source_target_pairs={{0,1},{1,2},{2,3},{3,4},{4,5},{5,6},{6,7},{7,0},{8,9},{9,10},{10,1... | collective-permute-start | bytes 1179656 | tf_op jit(solution)/shard_map/ppermute | solution.py:97
  289.7 20.5 %collective-permute-start.8 = (bf16[4,32,1536]{2,1,0:T(8,128)(2,1)S(1)}, bf16[4,32,1536]{2,1,0:T(8,128)(2,1)S(1)}, u32[]{:S(2)}, u32[]{:S(2)}) collective-permute-start(bf16[4,32,1536]{2,1,0:T(8,128)(2,1)S(1)} %collective-permute-done.7), channel_id=1, source_target_pairs={{0,1},{1,2},{2,3},{3,4},{4,5},{5,6},{6,7},{7,0},{8,9},{9,10},{10,1... | collective-permute-start | bytes 1179656 | tf_op jit(solution)/shard_map/ppermute | solution.py:97
  311.0 13.0 %collective-permute-start.9 = (bf16[4,32,1536]{2,1,0:T(8,128)(2,1)S(1)}, bf16[4,32,1536]{2,1,0:T(8,128)(2,1)S(1)}, u32[]{:S(2)}, u32[]{:S(2)}) collective-permute-start(bf16[4,32,1536]{2,1,0:T(8,128)(2,1)S(1)} %collective-permute-done.8), channel_id=1, source_target_pairs={{0,1},{1,2},{2,3},{3,4},{4,5},{5,6},{6,7},{7,0},{8,9},{9,10},{10,1... | collective-permute-start | bytes 1179656 | tf_op jit(solution)/shard_map/ppermute | solution.py:97
  324.7 12.1 %collective-permute-start.10 = (bf16[4,32,1536]{2,1,0:T(8,128)(2,1)S(1)}, bf16[4,32,1536]{2,1,0:T(8,128)(2,1)S(1)}, u32[]{:S(2)}, u32[]{:S(2)}) collective-permute-start(bf16[4,32,1536]{2,1,0:T(8,128)(2,1)S(1)} %collective-permute-done.9), channel_id=1, source_target_pairs={{0,1},{1,2},{2,3},{3,4},{4,5},{5,6},{6,7},{7,0},{8,9},{9,10},{10,1... | collective-permute-start | bytes 1179656 | tf_op jit(solution)/shard_map/ppermute | solution.py:97
  337.6 11.2 collective-permute-start.11
  349.5 10.6 collective-permute-start.12
  360.0 10.8 collective-permute-start.13
  360.1 50.8 %all-gather.17.cloned.1.call-start = ((), (), s32[]{:S(2)}) async-start(), calls=%async_computation.25 | async-start | bytes 2621440 | tf_op jit(solution)/shard_map/all_gather | solution.py:115
  379.2 65.6 %reduce-scatter.28.cloned.1.call-start = ((), (), s32[]{:S(2)}) async-start(), calls=%async_computation.35 | async-start | bytes 2621440 | tf_op jit(solution)/shard_map/reduce_scatter | solution.py:57
  403.0 75.8 %reduce-scatter.24.cloned.1.call-start = ((), (), s32[]{:S(2)}) async-start(), calls=%async_computation.32 | async-start | bytes 2621440 | tf_op jit(solution)/shard_map/reduce_scatter | solution.py:57
  425.2 87.5 %reduce-scatter.22.cloned.1.call-start = ((), (), s32[]{:S(2)}) async-start(), calls=%async_computation.31 | async-start | bytes 2621440 | tf_op jit(solution)/shard_map/reduce_scatter | solution.py:57
  430.3 108.6 %all-gather.25.cloned.1.call-start = ((), (), s32[]{:S(2)}) async-start(), calls=%async_computation.33 | async-start | bytes 2621440 | tf_op jit(solution)/shard_map/all_gather | solution.py:115
  516.1 46.9 %all-gather.27.cloned.1.call-start = ((), (), s32[]{:S(2)}) async-start(), calls=%async_computation.36 | async-start | bytes 2621440 | tf_op jit(solution)/shard_map/all_gather | solution.py:115
  516.7 154.1 %reduce-scatter.42.cloned.1.call-start = ((), (), s32[]{:S(2)}) async-start(), calls=%async_computation.43 | async-start | bytes 1769472 | tf_op jit(solution)/shard_map/reduce_scatter | solution.py:199
  524.4 174.4 %reduce-scatter.44.cloned.1.call-start = ((), (), s32[]{:S(2)}) async-start(), calls=%async_computation.44 | async-start | bytes 1769472 | tf_op jit(solution)/shard_map/reduce_scatter | solution.py:57
  531.0 235.2 %reduce-scatter.40.cloned.1.call-start = ((), (), s32[]{:S(2)}) async-start(), calls=%async_computation.42 | async-start | bytes 1769472 | tf_op jit(solution)/shard_map/reduce_scatter | solution.py:199
  537.9 293.0 %reduce-scatter.36.cloned.1.call-start = ((), (), s32[]{:S(2)}) async-start(), calls=%async_computation.40 | async-start | bytes 589824 | tf_op jit(solution)/shard_map/reduce_scatter | solution.py:199
  629.8 266.0 %reduce-scatter.34.cloned.1.call-start = ((), (), s32[]{:S(2)}) async-start(), calls=%async_computation.39 | async-start | bytes 589824 | tf_op jit(solution)/shard_map/reduce_scatter | solution.py:199
  636.0 326.2 %reduce-scatter.32.cloned.1.call-start = ((), (), s32[]{:S(2)}) async-start(), calls=%async_computation.38 | async-start | bytes 1179648 | tf_op jit(solution)/shard_map/reduce_scatter | solution.py:199
  649.7 378.8 %reduce-scatter.38.cloned.1.call-start = ((), (), s32[]{:S(2)}) async-start(), calls=%async_computation.41 | async-start | bytes 1179648 | tf_op jit(solution)/shard_map/reduce_scatter | solution.py:57
  654.1 407.4 %reduce-scatter.30.cloned.1.call-start = ((), (), s32[]{:S(2)}) async-start(), calls=%async_computation.37 | async-start | bytes 2621440 | tf_op jit(solution)/shard_map/reduce_scatter | solution.py:57
  659.1 436.9 %reduce-scatter.26.cloned.1.call-start = ((), (), s32[]{:S(2)}) async-start(), calls=%async_computation.34 | async-start | bytes 2621440 | tf_op jit(solution)/shard_map/reduce_scatter | solution.py:57
  664.9 478.1 %reduce-scatter.18.cloned.1.call-start = ((), (), s32[]{:S(2)}) async-start(), calls=%async_computation.27 | async-start | bytes 2621440 | tf_op jit(solution)/shard_map/reduce_scatter | solution.py:57
  670.9 95.4 %all-to-all-start.6 = ((bf16[4,32,768]{2,1,0:T(8,128)(2,1)}), bf16[4,32,768]{2,1,0:T(8,128)(2,1)S(1)}, u32[]{:S(2)}, u32[]{:S(2)}) async-start(bf16[4,32,768]{2,1,0:T(8,128)(2,1)} %reduce-scatter.42.cloned.1.call-done), calls=%async_computation.20 | async-start | bytes 393216 | tf_op jit(solution)/shard_map/all_to_all | solution.py:200
  766.3 8.7 all-to-all-start.5
  770.4 325.6 %copy-start.1 = (bf16[2,1,256,1024]{3,2,1,0:T(8,128)(2,1)S(1)}, bf16[2,1,256,1024]{3,2,1,0:T(8,128)(2,1)}, u32[]{:S(2)}) copy-start(bf16[2,1,256,1024]{3,2,1,0:T(8,128)(2,1)} %param.14) | copy-start | bytes 3145732
  770.4 325.6 %copy-start.83 = (f32[1024]{0:T(1024)S(1)}, f32[1024]{0:T(1024)}, u32[]{:S(2)}) copy-start(f32[1024]{0:T(1024)} %copy-done.82) | copy-start | bytes 12292
  770.4 325.6 %copy-start.95 = (f32[256]{0:T(256)S(1)}, f32[256]{0:T(256)}, u32[]{:S(2)}) copy-start(f32[256]{0:T(256)} %copy-done.94) | copy-start | bytes 3076
  770.5 325.6 %copy-start.103 = (f32[256]{0:T(256)S(1)}, f32[256]{0:T(256)}, u32[]{:S(2)}) copy-start(f32[256]{0:T(256)} %copy-done.102) | copy-start | bytes 3076
  830.9 64.9 %all-to-all-start.4 = ((bf16[4,32,256]{2,1,0:T(8,128)(2,1)}), bf16[4,32,256]{2,1,0:T(8,128)(2,1)S(1)}, u32[]{:S(2)}, u32[]{:S(2)}) async-start(bf16[4,32,256]{2,1,0:T(8,128)(2,1)} %reduce-scatter.36.cloned.1.call-done), calls=%async_computation.15 | async-start | bytes 131072 | tf_op jit(solution)/shard_map/all_to_all | solution.py:200
  895.8 7.4 all-to-all-start.3
  962.2 68.0 %all-to-all-start.2 = ((bf16[4,32,512]{2,1,0:T(8,128)(2,1)}), bf16[4,32,512]{2,1,0:T(8,128)(2,1)S(1)}, u32[]{:S(2)}, u32[]{:S(2)}) async-start(bf16[4,32,512]{2,1,0:T(8,128)(2,1)} %reduce-scatter.32.cloned.1.call-done), calls=%async_computation.11 | async-start | bytes 262144 | tf_op jit(solution)/shard_map/all_to_all | solution.py:200
  (149 other events, 3687.2 us)
Sparse Core Ops, SparseCore 0:
  58.0 23.1 all-gather.12
  82.8 21.8 all-gather.20
  106.8 41.9 all-gather.14
  196.8 27.2 reduce-scatter.19
  226.6 31.4 reduce-scatter.15
  260.1 54.3 all-gather.18
  316.6 21.7 all-gather.30
  339.9 22.5 all-gather.22
  364.1 22.5 all-gather.28
  388.2 22.6 all-gather.16
  413.4 31.3 reduce-scatter.27
  447.3 31.4 reduce-scatter.23
  481.3 31.4 reduce-scatter.21
  516.3 22.5 all-gather.24
  540.4 22.5 all-gather.26
  566.7 64.8 reduce-scatter.41
  634.9 63.8 reduce-scatter.43
  702.4 63.7 reduce-scatter.39
  769.6 61.2 reduce-scatter.35
  834.5 61.3 reduce-scatter.33
  899.3 62.8 reduce-scatter.31
  966.0 62.5 reduce-scatter.37
  1031.1 30.4 reduce-scatter.29
  1064.6 31.3 reduce-scatter.25
  1098.6 31.5 reduce-scatter.17
